TPU v7x, 128 devices: a whole 4x4x4 slice. The times are simulated.
128 devices in a mesh: pool: 4 (over y), seq: 32 (over x, z, core).
Axes of the slice: x: 4, y: 4, z: 4, core: 2. Of those that a mesh axis runs over, the one named last changes fastest.
Arguments:
- pool_kv: bfloat16 [16, 4096, 1024], P('pool', 'seq'), may hold values from -4 to 4
- span_home: int32 [12], replicated, may hold values from 0 to 15, as said below
- span_order: int32 [4, 3], P('pool'), may hold values from 0 to 11, as said below
- chosen: int32 [4, 14], P('pool'), may hold values from 0 to 95, as said below
- fresh_q: bfloat16 [4, 1792, 6144], P('pool', 'seq'), may hold values from -300 to 300
- fresh_kv: bfloat16 [4, 1792, 1024], P('pool', 'seq'), may hold values from -5 to 5
Outputs:
- attended: bfloat16 [4, 1792, 6144], P('pool', 'seq')
- decode_kv: bfloat16 [4, 32, 4, 96, 1024], P('pool', 'seq')
Inputs may be any that keep to these rules, and one draw needn't show every extreme that they name: `span_home`: all entries differ; home // 4 is the replica of a passage, and the 3 passages r * 3 to r * 3 + 2 of request r lie on different replicas; some replica holds a passage of every request. `span_order`: row r orders the passages r * 3 to r * 3 + 2. `chosen`: each row lists 14 different blocks in rising order; block k holds positions k * 128 to k * 128 + 127.
All inputs are finite; a program needn't handle non-finite values.
Results may differ from a plain program's by a relative error of at most 0.0035.
Values may be sent and summed in bfloat16 or wider, within the bound.
A program may use at most 192 MiB of HBM per device.

v0:
```python
import math
import jax
import jax.numpy as jnp
from jax import lax
from jax.sharding import PartitionSpec as P

KV_HEADS = 4
HEAD_DIM = 128
masked_low = -1e30


def patch_rows(values, positions, picked, fresh_all, block_len):
    block_ids = positions // block_len
    offsets = positions % block_len
    matches = block_ids[..., None] == picked
    is_fresh = jnp.any(matches, axis=-1)
    slot_ids = jnp.sum(jnp.where(matches, jnp.arange(picked.shape[0], dtype=jnp.int32), 0), axis=-1)
    source = (slot_ids * block_len + offsets).reshape(-1)
    rows_new = jnp.take(fresh_all, source, axis=0).reshape(values.shape)
    return jnp.where(is_fresh[..., None], rows_new, values)


def fold_keys(state_in, shard_piece, queries, query_pos, span_len):
    span_count, piece_rows, kv_width = shard_piece.shape
    key_pos = (
        jnp.arange(span_count, dtype=jnp.int32)[:, None] * span_len
        + jnp.arange(piece_rows, dtype=jnp.int32)[None, :]
    )
    kv_heads, query_rows, head_dim = queries.shape
    flattened = shard_piece.reshape(span_count * piece_rows, kv_heads, 2, head_dim)
    keys_all = flattened[:, :, 0]
    values_all = flattened[:, :, 1]
    pos_all = key_pos.reshape(-1)
    key_count = span_count * piece_rows
    step_len = math.gcd(key_count, 512)
    inv_root = head_dim ** (-0.5)

    def one_block(state_now, turn_at):
        running_max, total_weight, weighted = state_now
        first_key = turn_at * step_len
        key_blk = lax.dynamic_slice_in_dim(keys_all, first_key, step_len, 0)
        value_blk = lax.dynamic_slice_in_dim(values_all, first_key, step_len, 0)
        pos_blk = lax.dynamic_slice_in_dim(pos_all, first_key, step_len, 0)
        scores = (
            jnp.einsum("hqd,khd->hqk", queries, key_blk, preferred_element_type=jnp.float32)
            * inv_root
        )
        allowed = pos_blk[None, None, :] <= query_pos[None, :, None]
        scores = jnp.where(allowed, scores, masked_low)
        newest = jnp.maximum(running_max, jnp.max(scores, axis=-1))
        weights = jnp.where(allowed, jnp.exp(scores - newest[..., None]), 0.0)
        factor = jnp.exp(running_max - newest)
        total_weight = total_weight * factor + jnp.sum(weights, axis=-1)
        weighted = weighted * factor[..., None] + jnp.einsum(
            "hqk,khd->hqd",
            weights.astype(jnp.bfloat16),
            value_blk,
            preferred_element_type=jnp.float32,
        )
        return ((newest, total_weight, weighted), None)

    state_out, _ = lax.scan(one_block, state_in, jnp.arange(key_count // step_len))
    return state_out


def shards(pool_kv, span_home, span_order, chosen, fresh_q, fresh_kv):
    pool_count = lax.axis_size("pool")
    seq_count = lax.axis_size("seq")
    replica = lax.axis_index("pool")
    my_seat = lax.axis_index("seq")
    slot_count, block_len, kv_width = pool_kv.shape
    span_count = span_order.shape[1]
    span_len = block_len * seq_count
    head_dim = HEAD_DIM
    kv_heads = KV_HEADS
    picked = chosen[0]
    span_total = span_home.shape[0]
    home_replica = span_home // slot_count
    home_slot = span_home % slot_count
    span_request = jnp.arange(span_total, dtype=jnp.int32) // span_count
    requests = jnp.arange(pool_count, dtype=jnp.int32)
    held = (home_replica == replica)[None, :] & (span_request[None, :] == requests[:, None])
    in_slot = home_slot[None, :, None] == jnp.arange(slot_count, dtype=jnp.int32)[None, None, :]
    selector = jnp.any(held[:, :, None] & in_slot, axis=1).astype(jnp.bfloat16)
    outgoing = jnp.einsum(
        "rk,ktc->rtc", selector, pool_kv, preferred_element_type=jnp.float32
    ).astype(jnp.bfloat16)
    arrived = lax.all_to_all(outgoing, "pool", split_axis=0, concat_axis=0, tiled=True)
    order_row = span_order[0]
    lookup = order_row[:, None] == jnp.arange(span_total, dtype=jnp.int32)[None, :]
    source_replica = jnp.sum(jnp.where(lookup, home_replica[None, :], 0), axis=1)
    chooser = (source_replica[:, None] == requests[None, :]).astype(jnp.bfloat16)
    cached = jnp.einsum("jp,ptc->jtc", chooser, arrived, preferred_element_type=jnp.float32).astype(
        jnp.bfloat16
    )
    fresh_all = lax.all_gather(fresh_kv[0], "seq", axis=0, tiled=True)
    block_ids = jnp.arange(span_count, dtype=jnp.int32)[:, None] * seq_count + my_seat
    local_pos = block_ids * block_len + jnp.arange(block_len, dtype=jnp.int32)[None, :]
    patched = patch_rows(cached, local_pos, picked, fresh_all, block_len)
    row_count = fresh_q.shape[1]
    q_width = fresh_q.shape[2]
    group = q_width // (kv_heads * head_dim)
    list_rows = my_seat * row_count + jnp.arange(row_count, dtype=jnp.int32)
    list_block = list_rows // block_len
    base_block = jnp.sum(
        jnp.where(
            list_block[:, None] == jnp.arange(picked.shape[0], dtype=jnp.int32)[None, :],
            picked[None, :],
            0,
        ),
        axis=1,
    )
    query_pos = base_block * block_len + list_rows % block_len
    queries = fresh_q[0].reshape(row_count, kv_heads, group, head_dim).transpose(1, 2, 0, 3)
    queries = queries.reshape(kv_heads, group * row_count, head_dim)
    pos_tiled = jnp.tile(query_pos, group)
    start_state = (
        jnp.full((kv_heads, group * row_count), masked_low, jnp.float32),
        jnp.zeros((kv_heads, group * row_count), jnp.float32),
        jnp.zeros((kv_heads, group * row_count, head_dim), jnp.float32),
    )
    final_state = fold_keys(
        start_state,
        lax.all_gather(patched, "seq", axis=1, tiled=True),
        queries,
        pos_tiled,
        span_len,
    )
    running_max, total_weight, weighted = final_state
    attended = (weighted / total_weight[..., None]).reshape(kv_heads, group, row_count, head_dim)
    attended = attended.transpose(2, 0, 1, 3).reshape(1, row_count, q_width).astype(jnp.bfloat16)
    per_group = kv_heads // pool_count
    run_len = block_len // seq_count
    laid = patched.reshape(span_count, seq_count, run_len, pool_count, per_group, 2 * head_dim)
    laid = laid.transpose(3, 1, 4, 0, 2, 5).reshape(
        pool_count, seq_count, per_group, span_count, run_len * 2 * head_dim
    )
    merged = laid.reshape(pool_count * seq_count, per_group, span_count, run_len * 2 * head_dim)
    landed = lax.all_to_all(merged, ("pool", "seq"), split_axis=0, concat_axis=0, tiled=True)
    landed = landed.reshape(pool_count, seq_count, per_group, span_count, run_len * 2 * head_dim)
    decoded = landed.transpose(2, 0, 3, 1, 4).reshape(
        per_group, 1, pool_count, span_count * seq_count, run_len * 2 * head_dim
    )
    return (attended, decoded)


def solution(mesh):
    in_specs = (
        P("pool", "seq", None),
        P(),
        P("pool", None),
        P("pool", None),
        P("pool", "seq", None),
        P("pool", "seq", None),
    )
    out_specs = (P("pool", "seq", None), P("pool", "seq", None, None, None))
    return jax.shard_map(shards, mesh=mesh, in_specs=in_specs, out_specs=out_specs, check_vma=False)
```

profile of v0, /device:TPU:1, one launch (start us, length us, event | category | flops | bytes accessed | tf_op | source)
XLA Modules:
  0.0 632.1 jit_solution(8040437564425881074)
XLA Ops:
  11.7 5.0 all-to-all-start
  17.5 42.0 %all-gather.6.cloned.1.call-done = bf16[1,1792,1024]{2,1,0:T(8,128)(2,1)} async-done(((bf16[1,56,1024]{2,1,0:T(8,128)(2,1)}), bf16[1,1792,1024]{2,1,0:T(8,128)(2,1)}) %all-gather.6.cloned.1.call-update) | async-done | bytes 3670032 | tf_op jit(solution)/shard_map/all_gather | solution.py:96
  59.5 5.3 gather_fusion
  71.5 7.2 %all-to-all-start.1 = ((bf16[128,1,3,1024]{3,2,1,0:T(4,128)(2,1)}), bf16[128,1,3,1024]{3,2,1,0:T(4,128)(2,1)S(1)}, u32[]{:S(2)}, u32[]{:S(2)}) async-start(bf16[128,1,3,1024]{3,2,1,0:T(4,128)(2,1)} %reshape.349), calls=%async_computation.1 | async-start | bytes 2097152 | tf_op jit(solution)/shard_map/all_to_all | solution.py:139
  81.1 27.9 %all-to-all-done.1 = bf16[128,1,3,1024]{3,2,1,0:T(4,128)(2,1)S(1)} async-done(((bf16[128,1,3,1024]{3,2,1,0:T(4,128)(2,1)}), bf16[128,1,3,1024]{3,2,1,0:T(4,128)(2,1)S(1)}, u32[]{:S(2)}, u32[]{:S(2)}) %all-to-all-start.1) | async-done | bytes 786464 | tf_op jit(solution)/shard_map/all_to_all | solution.py:139
  110.2 60.9 %all-gather.4.cloned.1.call-done = bf16[3,4096,1024]{2,1,0:T(8,128)(2,1)} async-done(((bf16[3,128,1024]{2,1,0:T(8,128)(2,1)}), bf16[3,4096,1024]{2,1,0:T(8,128)(2,1)}) %all-gather.4.cloned.1.call-update) | async-done | bytes 25165840 | tf_op jit(solution)/shard_map/all_gather | solution.py:124
  171.1 40.5 %reshape.332 = bf16[12288,4,2,128]{3,2,1,0:T(2,128)(2,1)} reshape(bf16[3,4096,1024]{2,1,0:T(8,128)(2,1)} %all-gather.4.cloned.1.call-done) | data formatting | bytes 50331648 | tf_op jit(solution)/shard_map/reshape | solution.py:30
  211.6 47.1 %fusion.38 = (bf16[12288,4,1,128]{3,2,1,0:T(2,128)(2,1)}, bf16[12288,4,1,128]{3,2,1,0:T(2,128)(2,1)}) fusion(bf16[12288,4,2,128]{3,2,1,0:T(2,128)(2,1)} %reshape.332), kind=kLoop, calls=%fused_computation.93 | loop fusion | bytes 50331648 | tf_op jit(solution)/shard_map/slice | solution.py:32
  258.7 27.3 %copy_bitcast_fusion = (bf16[12288,4,128]{2,0,1:T(8,128)(2,1)}, bf16[12288,4,128]{2,0,1:T(8,128)(2,1)}) fusion(bf16[12288,4,1,128]{3,2,1,0:T(2,128)(2,1)} %get-tuple-element.129, bf16[12288,4,1,128]{3,2,1,0:T(2,128)(2,1)} %get-tuple-element.130), kind=kLoop, calls=%fused_computation.24 | loop fusion | bytes 50331648 | tf_op jit(solution)/shard_map/squeeze | solution.py:32
  286.1 337.2 %while.15 = (s32[]{:T(128)}, f32[4,672]{1,0:T(4,128)S(1)}, f32[4,672]{1,0:T(4,128)S(1)}, f32[4,672,128]{2,1,0:T(8,128)S(1)}, s32[24]{0:T(128)S(1)}, /*index=5*/s...) while((s32[]{:T(128)}, f32[4,672]{1,0:T(4,128)S(1)}, ...), condition=%wide.region_8.9_spmd.clone, body=%wide.region_5.8_spmd.clone.sunk | while | flops 723924096 | bytes 44590032 | solution.py:62
  287.9 4.5 fusion.50
  292.4 4.4 fusion.51
  301.9 4.5 fusion.50
  306.4 4.4 fusion.51
  316.0 4.5 fusion.50
  320.5 4.4 fusion.51
  330.0 4.5 fusion.50
  334.5 4.4 fusion.51
  344.1 4.5 fusion.50
  358.1 4.5 fusion.50
  362.6 4.4 fusion.51
  372.2 4.5 fusion.50
  376.7 4.4 fusion.51
  386.2 4.5 fusion.50
  390.7 4.4 fusion.51
  400.3 4.5 fusion.50
  404.8 4.4 fusion.51
  414.3 4.5 fusion.50
  418.8 4.4 fusion.51
  428.4 4.5 fusion.50
  442.4 4.5 fusion.50
  446.9 4.4 fusion.51
  456.5 4.5 fusion.50
  461.0 4.4 fusion.51
  470.5 4.5 fusion.50
  475.0 4.4 fusion.51
  484.6 4.5 fusion.50
  498.6 4.5 fusion.50
  512.7 4.5 fusion.50
  517.2 4.4 fusion.51
  526.7 4.5 fusion.50
  531.2 4.4 fusion.51
  540.8 4.5 fusion.50
  554.8 4.5 fusion.50
  568.9 4.5 fusion.50
  582.9 4.5 fusion.50
  597.0 4.5 fusion.50
  611.0 4.5 fusion.50
  (331 shorter events, 167.1 us)
Async XLA Ops:
  7.2 2.3 copy-start
  7.2 9.6 %copy-start.4 = (s32[1,14]{1,0:T(1,128)S(1)}, s32[1,14]{1,0:T(1,128)}, u32[]{:S(2)}) copy-start(s32[1,14]{1,0:T(1,128)} %param.11) | copy-start | bytes 172
  7.2 10.2 %copy-start.5 = (s32[1,3]{1,0:T(1,128)S(1)}, s32[1,3]{1,0:T(1,128)}, u32[]{:S(2)}) copy-start(s32[1,3]{1,0:T(1,128)} %param.10) | copy-start | bytes 40
  7.2 52.3 %all-gather.6.cloned.1.call-start = ((), (), s32[]{:S(2)}) async-start(), calls=%async_computation.3 | async-start | bytes 3784704 | tf_op jit(solution)/shard_map/all_gather | solution.py:96
  11.7 53.2 %all-to-all-start = ((bf16[4,128,1024]{2,1,0:T(8,128)(2,1)}), bf16[4,128,1024]{2,1,0:T(8,128)(2,1)S(1)}, u32[]{:S(2)}, u32[]{:S(2)}) async-start(bf16[4,128,1024]{2,1,0:T(8,128)(2,1)} %copy.49), calls=%async_computation | async-start | bytes 2097152 | tf_op jit(solution)/shard_map/all_to_all | solution.py:88
  16.6 154.5 %all-gather.4.cloned.1.call-start = ((), (), s32[]{:S(2)}) async-start(), calls=%async_computation.2 | async-start | bytes 25952256 | tf_op jit(solution)/shard_map/all_gather | solution.py:124
  71.5 37.4 %all-to-all-start.1 = ((bf16[128,1,3,1024]{3,2,1,0:T(4,128)(2,1)}), bf16[128,1,3,1024]{3,2,1,0:T(4,128)(2,1)S(1)}, u32[]{:S(2)}, u32[]{:S(2)}) async-start(bf16[128,1,3,1024]{3,2,1,0:T(4,128)(2,1)} %reshape.349), calls=%async_computation.1 | async-start | bytes 2097152 | tf_op jit(solution)/shard_map/all_to_all | solution.py:139
  258.7 27.3 %copy-start.3 = (f32[4,672,128]{2,1,0:T(8,128)S(1)}, f32[4,672,128]{2,1,0:T(8,128)}, u32[]{:S(2)}) copy-start(f32[4,672,128]{2,1,0:T(8,128)} %custom-call.2) | copy-start | bytes 4128772
  292.4 4.4 copy-start.2
  306.4 4.4 copy-start.2
  320.5 4.4 copy-start.2
  334.5 4.4 copy-start.2
  348.6 4.4 copy-start.2
  362.6 4.4 copy-start.2
  376.7 4.4 copy-start.2
  390.7 4.4 copy-start.2
  404.8 4.4 copy-start.2
  418.8 4.4 copy-start.2
  432.9 4.4 copy-start.2
  446.9 4.4 copy-start.2
  461.0 4.4 copy-start.2
  475.0 4.4 copy-start.2
  489.1 4.4 copy-start.2
  503.1 4.4 copy-start.2
  517.2 4.4 copy-start.2
  531.2 4.4 copy-start.2
  545.3 4.4 copy-start.2
  559.3 4.4 copy-start.2
  573.4 4.4 copy-start.2
  587.4 4.4 copy-start.2
  601.5 4.4 copy-start.2
  615.5 4.4 copy-start.2
  623.3 2.0 copy-start.1
Sparse Core Ops, SparseCore 0:
  10.3 49.2 all-gather.5
  69.1 102.0 all-gather.3
where the time goes:
time: 636 us; the launch traced here: 632 us
  matrix products  191 us (30%)
  local copies, waits for them, and re-layouts  150 us (24%)
  waiting for transfers between devices  131 us (21%)
  other arithmetic  114 us (18%)
  loops' own time  18.3 us (3%)
  between operations  14.3 us (2%)
  starting transfers between devices  12.2 us (2%)
    dot_general x24, matrix products, one_block(): jnp.einsum('hqd,khd->hqk', queries, key_blk, preferred_element_type=jnp.f...  108 us
    reduce_sum x24, other arithmetic, one_block(): total_weight = total_weight * factor + jnp.sum(weights, axis=-1)  105 us
    dot_general x24, matrix products, one_block(): jnp.einsum('hqk,khd->hqd', weights.astype(jnp.bfloat16), value_blk, prefe...  79.2 us
    all_gather x1, waiting for transfers between devices, shards(): lax.all_gather(patched, 'seq', axis=1, tiled=True)  60.9 us
    slice x1, local copies, waits for them, and re-layouts, fold_keys(): values_all = flattened[:, :, 1]  47.1 us
    all_gather x1, waiting for transfers between devices, shards(): fresh_all = lax.all_gather(fresh_kv[0], 'seq', axis=0, tiled=True)  42 us
    reshape x1, local copies, waits for them, and re-layouts, fold_keys(): shard_piece.reshape(span_count * piece_rows, kv_heads, 2, head_dim)  40.5 us
    all_to_all x1, waiting for transfers between devices, shards(): lax.all_to_all(merged, ('pool', 'seq'), split_axis=0, concat_axis=0, tile...  27.9 us
  transfers between devices with their start and end apart: 4, of which 3 were waited for; matrix products, arithmetic and copies ran while one was open for 3% of the time, Pallas kernels for 0%

commit v1 on v0

--- a/solution.py
+++ b/solution.py
@@ -121,7 +121,7 @@
     )
     final_state = fold_keys(
         start_state,
-        lax.all_gather(patched, "seq", axis=1, tiled=True),
+        jnp.concatenate(lax.all_gather(patched, "seq"), axis=1),
         queries,
         pos_tiled,
         span_len,

time: 636 us -> 608 us (0.956)
  local copies, waits for them, and re-layouts: 150 us -> 121 us
    slice x1 -> x0, local copies, waits for them, and re-layouts: 47.1 us -> none  [fold_keys(): values_all = flattened[:, :, 1]]
    another operation x0 -> x1, local copies, waits for them, and re-layouts: none -> 35.5 us  [fold_keys(): shard_piece.reshape(span_count * piece_rows, kv_heads, 2, head_dim)]
    squeeze x1, local copies, waits for them, and re-layouts: 27.3 us -> 17.8 us  [fold_keys(): values_all = flattened[:, :, 1]]
    reshape x1, local copies, waits for them, and re-layouts: 40.5 us -> 32 us  [shards(): jnp.concatenate(lax.all_gather(patched, 'seq'), axis=1)]
where the time goes in v1:
time: 608 us; the launch traced here: 604 us
  matrix products  192 us (32%)
  waiting for transfers between devices  131 us (22%)
  local copies, waits for them, and re-layouts  121 us (20%)
  other arithmetic  114 us (19%)
  loops' own time  18.3 us (3%)
  between operations  14.3 us (2%)
  starting transfers between devices  12.2 us (2%)
    dot_general x24, matrix products, one_block(): jnp.einsum('hqd,khd->hqk', queries, key_blk, preferred_element_type=jnp.f...  108 us
    reduce_sum x24, other arithmetic, one_block(): total_weight = total_weight * factor + jnp.sum(weights, axis=-1)  105 us
    dot_general x24, matrix products, one_block(): jnp.einsum('hqk,khd->hqd', weights.astype(jnp.bfloat16), value_blk, prefe...  80.7 us
    all_gather x1, waiting for transfers between devices, shards(): lax.all_gather(patched, 'seq')  60.9 us
    all_gather x1, waiting for transfers between devices, shards(): fresh_all = lax.all_gather(fresh_kv[0], 'seq', axis=0, tiled=True)  42 us
    another operation x1, local copies, waits for them, and re-layouts, fold_keys(): shard_piece.reshape(span_count * piece_rows, kv_heads, 2, head_dim)  35.5 us
    reshape x1, local copies, waits for them, and re-layouts, shards(): jnp.concatenate(lax.all_gather(patched, 'seq'), axis=1)  32 us
    all_to_all x1, waiting for transfers between devices, shards(): lax.all_to_all(merged, ('pool', 'seq'), split_axis=0, concat_axis=0, tile...  27.9 us
  transfers between devices with their start and end apart: 4, of which 3 were waited for; matrix products, arithmetic and copies ran while one was open for 3% of the time, Pallas kernels for 0%

profile of v1, /device:TPU:1, one launch (start us, length us, event | category | flops | bytes accessed | tf_op | source)
XLA Modules:
  0.0 603.7 jit_solution(9825637824606594888)
XLA Ops:
  11.7 5.0 all-to-all-start
  17.5 42.0 %all-gather.5.cloned.1.call-done = bf16[1,1792,1024]{2,1,0:T(8,128)(2,1)} async-done(((bf16[1,56,1024]{2,1,0:T(8,128)(2,1)}), bf16[1,1792,1024]{2,1,0:T(8,128)(2,1)}) %all-gather.5.cloned.1.call-update) | async-done | bytes 3670032 | tf_op jit(solution)/shard_map/all_gather | solution.py:96
  59.5 5.3 gather_fusion
  71.5 7.2 %all-to-all-start.1 = ((bf16[128,1,3,1024]{3,2,1,0:T(4,128)(2,1)}), bf16[128,1,3,1024]{3,2,1,0:T(4,128)(2,1)S(1)}, u32[]{:S(2)}, u32[]{:S(2)}) async-start(bf16[128,1,3,1024]{3,2,1,0:T(4,128)(2,1)} %reshape.350), calls=%async_computation.1 | async-start | bytes 2097152 | tf_op jit(solution)/shard_map/all_to_all | solution.py:139
  81.1 27.9 %all-to-all-done.1 = bf16[128,1,3,1024]{3,2,1,0:T(4,128)(2,1)S(1)} async-done(((bf16[128,1,3,1024]{3,2,1,0:T(4,128)(2,1)}), bf16[128,1,3,1024]{3,2,1,0:T(4,128)(2,1)S(1)}, u32[]{:S(2)}, u32[]{:S(2)}) %all-to-all-start.1) | async-done | bytes 786464 | tf_op jit(solution)/shard_map/all_to_all | solution.py:139
  110.2 60.9 %all-gather.7.cloned.1.call-done = bf16[96,128,1024]{2,1,0:T(8,128)(2,1)} async-done(((bf16[3,128,1024]{2,1,0:T(8,128)(2,1)}), bf16[96,128,1024]{2,1,0:T(8,128)(2,1)}) %all-gather.7.cloned.1.call-update) | async-done | bytes 25165840 | tf_op jit(solution)/shard_map/all_gather | solution.py:124
  171.1 32.0 %copy.55 = bf16[3,32,128,1024]{2,1,0,3:T(8,128)(2,1)} copy(bf16[3,32,128,1024]{3,2,0,1:T(8,128)(2,1)} %bitcast.79) | data formatting | bytes 50331648 | tf_op jit(solution)/shard_map/reshape | solution.py:124
  203.1 35.5 %reshape_reshape.6 = bf16[12288,4,2,128]{0,3,2,1:T(8,128)(2,1)} reshape(bf16[3,32,128,1024]{2,1,0,3:T(8,128)(2,1)} %copy.55) | data formatting | bytes 50331648 | tf_op jit(solution)/shard_map/reshape;reshape | solution.py:30
  238.6 17.8 %slice_bitcast_fusion = (bf16[12288,4,128]{0,2,1:T(8,128)(2,1)}, bf16[12288,4,128]{0,2,1:T(8,128)(2,1)}) fusion(bf16[12288,4,2,128]{0,3,2,1:T(8,128)(2,1)} %reshape_reshape.6), kind=kLoop, calls=%fused_computation.24 | loop fusion | bytes 50331648 | tf_op jit(solution)/shard_map/squeeze | solution.py:32
  256.5 338.3 %while.15 = (s32[]{:T(128)}, f32[4,672]{1,0:T(4,128)S(1)}, f32[4,672]{1,0:T(4,128)S(1)}, f32[4,672,128]{2,1,0:T(8,128)S(1)}, s32[24]{0:T(128)S(1)}, /*index=5*/s...) while((s32[]{:T(128)}, f32[4,672]{1,0:T(4,128)S(1)}, ...), condition=%wide.region_8.9_spmd.clone, body=%wide.region_5.8_spmd.clone.sunk | while | flops 723924096 | bytes 44590032 | solution.py:62
  258.3 4.5 fusion.49
  262.8 4.4 fusion.50
  272.4 4.5 fusion.49
  276.9 4.4 fusion.50
  286.5 4.5 fusion.49
  291.0 4.4 fusion.50
  300.6 4.5 fusion.49
  305.1 4.4 fusion.50
  314.7 4.5 fusion.49
  328.8 4.5 fusion.49
  333.3 4.4 fusion.50
  342.9 4.5 fusion.49
  347.4 4.4 fusion.50
  357.0 4.5 fusion.49
  371.1 4.5 fusion.49
  375.6 4.4 fusion.50
  385.2 4.5 fusion.49
  399.3 4.5 fusion.49
  403.8 4.4 fusion.50
  413.4 4.5 fusion.49
  417.9 4.4 fusion.50
  427.5 4.5 fusion.49
  432.0 4.4 fusion.50
  441.6 4.5 fusion.49
  446.1 4.4 fusion.50
  455.7 4.5 fusion.49
  469.8 4.5 fusion.49
  474.3 4.4 fusion.50
  483.9 4.5 fusion.49
  488.4 4.4 fusion.50
  498.0 4.5 fusion.49
  512.1 4.5 fusion.49
  516.6 4.4 fusion.50
  526.2 4.5 fusion.49
  540.3 4.5 fusion.49
  554.3 4.5 fusion.49
  568.4 4.5 fusion.49
  582.5 4.5 fusion.49
  (331 shorter events, 168.7 us)
Async XLA Ops:
  7.2 2.3 copy-start
  7.2 9.6 %copy-start.4 = (s32[1,14]{1,0:T(1,128)S(1)}, s32[1,14]{1,0:T(1,128)}, u32[]{:S(2)}) copy-start(s32[1,14]{1,0:T(1,128)} %param.11) | copy-start | bytes 172
  7.2 10.2 %copy-start.5 = (s32[1,3]{1,0:T(1,128)S(1)}, s32[1,3]{1,0:T(1,128)}, u32[]{:S(2)}) copy-start(s32[1,3]{1,0:T(1,128)} %param.10) | copy-start | bytes 40
  7.2 52.3 %all-gather.5.cloned.1.call-start = ((), (), s32[]{:S(2)}) async-start(), calls=%async_computation.2 | async-start | bytes 3784704 | tf_op jit(solution)/shard_map/all_gather | solution.py:96
  11.7 53.2 %all-to-all-start = ((bf16[4,128,1024]{2,1,0:T(8,128)(2,1)}), bf16[4,128,1024]{2,1,0:T(8,128)(2,1)S(1)}, u32[]{:S(2)}, u32[]{:S(2)}) async-start(bf16[4,128,1024]{2,1,0:T(8,128)(2,1)} %copy.52), calls=%async_computation | async-start | bytes 2097152 | tf_op jit(solution)/shard_map/all_to_all | solution.py:88
  16.6 154.5 %all-gather.7.cloned.1.call-start = ((), (), s32[]{:S(2)}) async-start(), calls=%async_computation.3 | async-start | bytes 25952256 | tf_op jit(solution)/shard_map/all_gather | solution.py:124
  71.5 37.4 %all-to-all-start.1 = ((bf16[128,1,3,1024]{3,2,1,0:T(4,128)(2,1)}), bf16[128,1,3,1024]{3,2,1,0:T(4,128)(2,1)S(1)}, u32[]{:S(2)}, u32[]{:S(2)}) async-start(bf16[128,1,3,1024]{3,2,1,0:T(4,128)(2,1)} %reshape.350), calls=%async_computation.1 | async-start | bytes 2097152 | tf_op jit(solution)/shard_map/all_to_all | solution.py:139
  238.6 17.9 %copy-start.3 = (f32[4,672,128]{2,1,0:T(8,128)S(1)}, f32[4,672,128]{2,1,0:T(8,128)}, u32[]{:S(2)}) copy-start(f32[4,672,128]{2,1,0:T(8,128)} %custom-call.2) | copy-start | bytes 4128772
  262.8 4.4 copy-start.2
  276.9 4.4 copy-start.2
  291.0 4.4 copy-start.2
  305.1 4.4 copy-start.2
  319.2 4.4 copy-start.2
  333.3 4.4 copy-start.2
  347.4 4.4 copy-start.2
  361.5 4.4 copy-start.2
  375.6 4.4 copy-start.2
  389.7 4.4 copy-start.2
  403.8 4.4 copy-start.2
  417.9 4.4 copy-start.2
  432.0 4.4 copy-start.2
  446.1 4.4 copy-start.2
  460.2 4.4 copy-start.2
  474.3 4.4 copy-start.2
  488.4 4.4 copy-start.2
  502.5 4.4 copy-start.2
  516.5 4.4 copy-start.2
  530.6 4.4 copy-start.2
  544.7 4.4 copy-start.2
  558.8 4.4 copy-start.2
  572.9 4.4 copy-start.2
  587.0 4.4 copy-start.2
  594.8 2.0 copy-start.1
Sparse Core Ops, SparseCore 0:
  10.3 49.2 all-gather.4
  69.1 102.0 all-gather.6
